TPU v7x, 32 devices: a whole 2x2x4 slice. The times are simulated.
32 devices in a mesh: group: 2 (over y), tm: 4 (over z), mp: 4 (over x, core).
Axes of the slice: x: 2, y: 2, z: 4, core: 2. Of those that a mesh axis runs over, the one named last changes fastest.
Arguments:
- latents: bfloat16 [2, 4, 256, 1536], P('group', 'tm'), parts along dimension 0, may hold values from -6 to 6
- gsd_table: float32 [8, 6, 1536], replicated, may hold values from -3 to 3
- gsd_bucket: int32 [2, 4], P('group', 'tm'), parts along dimension 0, may hold values from 0 to 7
- clearest: int32 [2], P('group'), parts along dimension 0, may hold values from 0 to 3, as said below
- clouds: int32 [2, 4, 256], P('group'), parts along dimension 0, may hold values from 0 to 1
- cross_query: bfloat16 [1536, 1536], P('tm', 'mp'), may hold values from -5 to 5
- cross_pairs: bfloat16 [1536, 2, 1536], P('tm', None, 'mp'), may hold values from -5 to 5
- cross_merge: bfloat16 [1536, 1536], P('mp', 'tm'), may hold values from -0.15625 to 0.15625
- time_triple: bfloat16 [1536, 3, 1536], P('tm', None, 'mp'), may hold values from -5 to 5
- time_merge: bfloat16 [1536, 1536], P('mp', 'tm'), may hold values from -0.15625 to 0.15625
Outputs:
- updated: bfloat16 [2, 4, 256, 1536], P('group', 'tm'), parts along dimension 0
There are 2 independent parts, one for each index of `group`. A program takes and returns all parts, laid end to end along the dimension named above; an argument that names none is the same for every part. Nothing has to cross between parts.
Inputs may be any that keep to these rules, and one draw needn't show every extreme that they name: clearest[s] is one of the stack's dates; that date has no cloudy token, and no date of stack s has fewer cloudy tokens.
All inputs are finite; a program needn't handle non-finite values.
Results may differ from a plain program's by a relative error of at most 0.014.
The roundings to bfloat16 on the way count: a program that leaves them out, or rounds other values in their place, can miss the bound.
Values may be sent and summed in bfloat16 or wider, within the bound.
A program may use at most 64 MiB of HBM per device.

v0:
```python
import jax
import jax.numpy as jnp
from jax import lax
from jax.sharding import PartitionSpec as P

HEAD_DIM = 64


def broadcast(block, axis, holder):
    block = jnp.where(lax.axis_index(axis) == holder, block, jnp.zeros_like(block))
    return lax.psum(block, axis)


def normalize(values):
    centre = jnp.mean(values, axis=-1, keepdims=True)
    shifted = values - centre
    variance = jnp.mean(shifted * shifted, axis=-1, keepdims=True)
    return shifted * lax.rsqrt(variance + 1e-06)


def softmax_rows(scores):
    highest = jnp.max(scores, axis=-1, keepdims=True)
    weights = jnp.exp(scores - highest)
    return weights / jnp.sum(weights, axis=-1, keepdims=True)


def shards(
    latents,
    gsd_table,
    gsd_bucket,
    clearest,
    clouds,
    cross_query,
    cross_pairs,
    cross_merge,
    time_triple,
    time_merge,
):
    stacks = latents.shape[0]
    seq_tokens = latents.shape[2]
    model_width = latents.shape[3]
    local_width = cross_query.shape[1]
    local_heads = local_width // HEAD_DIM
    buckets = gsd_table.shape[0]
    scale_factor = HEAD_DIM ** (-0.5)
    my_buckets = gsd_bucket.reshape(stacks)
    one_hot = (my_buckets[:, None] == jnp.arange(buckets, dtype=jnp.int32)[None, :]).astype(
        jnp.float32
    )
    modulation = jnp.dot(
        one_hot, gsd_table.reshape(buckets, 6 * model_width), precision=lax.Precision.HIGHEST
    ).reshape(stacks, 6, 1, 1, model_width)
    values = latents.astype(jnp.float32)
    normed = (normalize(values) * (1.0 + modulation[:, 1]) + modulation[:, 0]).astype(jnp.bfloat16)
    full_query, full_pairs, full_merge, full_triple, full_time = (
        lax.all_gather(cross_query, "tm", axis=0, tiled=True),
        lax.all_gather(cross_pairs, "tm", axis=0, tiled=True),
        lax.all_gather(cross_merge, "tm", axis=1, tiled=True),
        lax.all_gather(time_triple, "tm", axis=0, tiled=True),
        lax.all_gather(time_merge, "tm", axis=1, tiled=True),
    )
    flat_rows = normed.reshape(stacks * seq_tokens, model_width)
    queries = jnp.dot(flat_rows, full_query, preferred_element_type=jnp.float32).astype(
        jnp.bfloat16
    )

    def project_reference(ref_rows):
        return jnp.einsum(
            "ld,dce->lce", ref_rows, full_pairs, preferred_element_type=jnp.float32
        ).astype(jnp.bfloat16)

    def empty_pairs(ref_rows):
        return jnp.zeros((ref_rows.shape[0], 2, local_width), jnp.bfloat16)

    position = lax.axis_index("tm")
    owner_date = clearest[0]
    local_pair = lax.cond(position == owner_date, project_reference, empty_pairs, normed[0, 0])
    key_pair = broadcast(local_pair, "tm", owner_date)
    pair_list = [key_pair]
    key_pairs = jnp.stack(pair_list)
    heads_query = queries.reshape(stacks, seq_tokens, local_heads, HEAD_DIM)
    heads_key = key_pairs[:, :, 0].reshape(stacks, seq_tokens, local_heads, HEAD_DIM)
    heads_value = key_pairs[:, :, 1].reshape(stacks, seq_tokens, local_heads, HEAD_DIM)
    scores = (
        jnp.einsum("sqhe,skhe->shqk", heads_query, heads_key, preferred_element_type=jnp.float32)
        * scale_factor
    )
    attn_weights = softmax_rows(scores).astype(jnp.bfloat16)
    attended = jnp.einsum(
        "shqk,skhe->sqhe", attn_weights, heads_value, preferred_element_type=jnp.float32
    ).astype(jnp.bfloat16)
    cross_terms = jnp.dot(
        attended.reshape(stacks * seq_tokens, local_width),
        full_merge,
        preferred_element_type=jnp.float32,
    )
    cross_sum = lax.psum(cross_terms.astype(jnp.bfloat16), "mp").astype(jnp.float32)
    middle = values + modulation[:, 2] * cross_sum.reshape(stacks, 1, seq_tokens, model_width)
    normed_two = (normalize(middle) * (1.0 + modulation[:, 4]) + modulation[:, 3]).astype(
        jnp.bfloat16
    )
    triple = jnp.einsum(
        "nd,dce->nce",
        normed_two.reshape(stacks * seq_tokens, model_width),
        full_triple,
        preferred_element_type=jnp.float32,
    ).astype(jnp.bfloat16)
    triple = triple.reshape(stacks, 1, seq_tokens, 3, local_width)
    patches = lax.all_to_all(triple, "tm", split_axis=2, concat_axis=1, tiled=True)
    date_count = patches.shape[1]
    patch_count = patches.shape[2]
    allowed = lax.dynamic_slice_in_dim(clouds == 0, position * patch_count, patch_count, 2)
    split_heads = patches.reshape(stacks, date_count, patch_count, 3, local_heads, HEAD_DIM)
    scores_time = (
        jnp.einsum(
            "sdphe,sfphe->sphdf",
            split_heads[:, :, :, 0],
            split_heads[:, :, :, 1],
            preferred_element_type=jnp.float32,
        )
        * scale_factor
    )
    visible = jnp.transpose(allowed, (0, 2, 1))[:, :, None, None, :]
    scores_time = jnp.where(visible, scores_time, -1e30)
    time_weights = softmax_rows(scores_time).astype(jnp.bfloat16)
    mixed_out = jnp.einsum(
        "sphdf,sfphe->sdphe",
        time_weights,
        split_heads[:, :, :, 2],
        preferred_element_type=jnp.float32,
    ).astype(jnp.bfloat16)
    mixed_out = mixed_out.reshape(stacks, date_count, patch_count, local_width)
    returned = lax.all_to_all(mixed_out, "tm", split_axis=1, concat_axis=2, tiled=True)
    time_terms = jnp.dot(
        returned.reshape(stacks * seq_tokens, local_width),
        full_time,
        preferred_element_type=jnp.float32,
    )
    time_sum = lax.psum(time_terms.astype(jnp.bfloat16), "mp").astype(jnp.float32)
    return (
        middle + modulation[:, 5] * time_sum.reshape(stacks, 1, seq_tokens, model_width)
    ).astype(jnp.bfloat16)


def solution(mesh):
    placed = (
        P("group", "tm", None, None),
        P(),
        P("group", "tm"),
        P("group"),
        P("group", None, None),
        P("tm", "mp"),
        P("tm", None, "mp"),
        P("mp", "tm"),
        P("tm", None, "mp"),
        P("mp", "tm"),
    )
    return jax.shard_map(
        shards, mesh=mesh, in_specs=placed, out_specs=P("group", "tm", None, None), check_vma=False
    )
```

profile of v0, /device:TPU:0, one launch (start us, length us, event | category | flops | bytes accessed | tf_op | source)
XLA Modules:
  0.0 375.0 jit_solution(14642475833497510122)
XLA Ops:
  6.5 2.0 copy.47
  8.7 0.7 all-gather.8.cloned.1.call-update
  10.1 0.3 fusion.26
  11.0 0.1 slice_reduce_fusion.1
  11.1 0.2 convert_reduce_fusion
  11.3 0.3 fusion.6
  11.7 0.4 fusion.19
  12.1 50.1 %all-gather.6.cloned.1.call-done = bf16[1536,2,384]{2,0,1:T(8,128)(2,1)} async-done(((bf16[384,2,384]{2,0,1:T(8,128)(2,1)}), bf16[1536,2,384]{2,0,1:T(8,128)(2,1)}) %all-gather.6.cloned.1.call-update) | async-done | bytes 2359312 | tf_op jit(solution)/shard_map/all_gather | solution.py:57
  62.2 0.8 select_bitcast_fusion
  63.1 0.5 all-gather.10.cloned.1.call-update
  63.7 29.4 %all-gather.8.cloned.1.call-done = bf16[1536,384]{1,0:T(8,128)(2,1)} async-done(((bf16[384,384]{1,0:T(8,128)(2,1)}), bf16[1536,384]{1,0:T(8,128)(2,1)}) %all-gather.8.cloned.1.call-update) | async-done | bytes 1179664 | tf_op jit(solution)/shard_map/all_gather | solution.py:56
  93.0 1.8 convolution_convert_fusion.5
  94.9 0.1 copy.49
  95.0 36.6 %all-reduce.4.cloned.1.call-done = bf16[1,256,2,384]{3,1,2,0:T(8,128)(2,1)} async-done(((bf16[1,256,2,384]{3,1,2,0:T(8,128)(2,1)}), bf16[1,256,2,384]{3,1,2,0:T(8,128)(2,1)}) %all-reduce.4.cloned.1.call-update) | async-done | bytes 393232 | tf_op jit(solution)/shard_map/psum | solution.py:11
  131.6 1.1 fusion.44
  132.7 0.1 copy.50
  132.8 0.1 copy.48
  133.0 0.7 fusion.45
  133.6 0.3 convolution_convert_fusion.6
  133.9 29.0 %all-gather.10.cloned.1.call-done = bf16[384,1536]{1,0:T(8,128)(2,1)} async-done(((bf16[384,384]{1,0:T(8,128)(2,1)}), bf16[384,1536]{1,0:T(8,128)(2,1)}) %all-gather.10.cloned.1.call-update) | async-done | bytes 1179664 | tf_op jit(solution)/shard_map/all_gather | solution.py:58
  162.9 2.7 convolution_convert_fusion.2
  165.7 0.0 all-gather.12.cloned.1.call-start
  165.7 0.5 all-gather.12.cloned.1.call-update
  166.2 33.6 %all-reduce.6.cloned.1.call-done = bf16[256,1536]{1,0:T(8,128)(2,1)} async-done(((bf16[256,1536]{1,0:T(8,128)(2,1)}), bf16[256,1536]{1,0:T(8,128)(2,1)}) %all-reduce.6.cloned.1.call-update) | async-done | bytes 786448 | tf_op jit(solution)/shard_map/psum | solution.py:97
  199.9 1.5 fusion.16
  201.4 0.4 multiply_reduce_fusion
  201.9 69.5 %all-gather.12.cloned.1.call-done = bf16[1536,3,384]{2,0,1:T(8,128)(2,1)} async-done(((bf16[384,3,384]{2,0,1:T(8,128)(2,1)}), bf16[1536,3,384]{2,0,1:T(8,128)(2,1)}) %all-gather.12.cloned.1.call-update) | async-done | bytes 3538960 | tf_op jit(solution)/shard_map/all_gather | solution.py:59
  271.4 3.2 fusion.12
  274.7 1.4 copy.52
  276.1 4.2 %all-to-all-start = ((bf16[1,1,256,3,384]{4,3,1,0,2:T(4,128)(2,1)}), bf16[1,1,256,3,384]{4,3,1,0,2:T(4,128)(2,1)}, u32[]{:S(2)}, u32[]{:S(2)}) async-start(bf16[1,1,256,3,384]{4,3,1,0,2:T(4,128)(2,1)} %copy.52), calls=%async_computation | async-start | bytes 1572864 | tf_op jit(solution)/shard_map/all_to_all | solution.py:109
  280.3 0.7 all-gather.14.cloned.1.call-update
  281.0 0.1 fusion.34
  281.1 31.1 %all-to-all-done = bf16[1,1,256,3,384]{4,3,1,0,2:T(4,128)(2,1)} async-done(((bf16[1,1,256,3,384]{4,3,1,0,2:T(4,128)(2,1)}), bf16[1,1,256,3,384]{4,3,1,0,2:T(4,128)(2,1)}, u32[]{:S(2)}, u32[]{:S(2)}) %all-to-all-start) | async-done | bytes 589856 | tf_op jit(solution)/shard_map/all_to_all | solution.py:109
  312.2 2.7 reshape.227
  315.0 1.1 fusion.43
  316.0 0.6 fusion.25
  316.6 0.3 copy.57
  317.0 0.1 fusion.46
  317.1 0.3 copy.58
  317.4 0.6 fusion.13
  318.0 0.1 copy.59
  318.1 1.0 reshape.221
  319.1 3.4 all-to-all-start.1
  322.5 0.0 all-reduce.8.cloned.1.call-start
  322.5 6.1 %all-to-all-done.1 = bf16[1,4,64,384]{3,2,0,1:T(8,128)(2,1)S(1)} async-done(((bf16[1,4,64,384]{3,2,0,1:T(8,128)(2,1)}), bf16[1,4,64,384]{3,2,0,1:T(8,128)(2,1)S(1)}, u32[]{:S(2)}, u32[]{:S(2)}) %all-to-all-start.1) | async-done | bytes 196640 | tf_op jit(solution)/shard_map/all_to_all | solution.py:133
  328.7 2.7 convolution_convert_fusion.1
  331.4 34.3 %all-reduce.8.cloned.1.call-done = bf16[256,1536]{1,0:T(8,128)(2,1)} async-done(((bf16[256,1536]{1,0:T(8,128)(2,1)}), bf16[256,1536]{1,0:T(8,128)(2,1)}) %all-reduce.8.cloned.1.call-update) | async-done | bytes 786448 | tf_op jit(solution)/shard_map/psum | solution.py:139
  365.8 2.4 fusion.10
  (29 shorter events, 0.4 us)
Async XLA Ops:
  6.5 3.5 copy-start
  6.5 4.6 %copy-start.1 = (bf16[1,1,256,1536]{3,2,1,0:T(8,128)(2,1)S(1)}, bf16[1,1,256,1536]{3,2,1,0:T(8,128)(2,1)}, u32[]{:S(2)}) copy-start(bf16[1,1,256,1536]{3,2,1,0:T(8,128)(2,1)} %param.12) | copy-start | bytes 2359300
  6.5 55.6 %all-gather.6.cloned.1.call-start = ((), (), s32[]{:S(2)}) async-start(), calls=%async_computation.2 | async-start | bytes 2949120 | tf_op jit(solution)/shard_map/all_gather | solution.py:57
  8.6 84.4 %all-gather.8.cloned.1.call-start = ((), (), s32[]{:S(2)}) async-start(), calls=%async_computation.4 | async-start | bytes 1474560 | tf_op jit(solution)/shard_map/all_gather | solution.py:56
  9.4 122.2 %all-reduce.4.cloned.1.call-start = ((), (), s32[]{:S(2)}) async-start(), calls=%async_computation.3 | async-start | bytes 786432 | tf_op jit(solution)/shard_map/psum | solution.py:11
  63.0 99.8 %all-gather.10.cloned.1.call-start = ((), (), s32[]{:S(2)}) async-start(), calls=%async_computation.5 | async-start | bytes 1474560 | tf_op jit(solution)/shard_map/all_gather | solution.py:58
  63.6 136.3 %all-reduce.6.cloned.1.call-start = ((), (), s32[]{:S(2)}) async-start(), calls=%async_computation.6 | async-start | bytes 1572864 | tf_op jit(solution)/shard_map/psum | solution.py:97
  165.7 105.8 %all-gather.12.cloned.1.call-start = ((), (), s32[]{:S(2)}) async-start(), calls=%async_computation.7 | async-start | bytes 4423680 | tf_op jit(solution)/shard_map/all_gather | solution.py:59
  199.9 1.6 copy-start.2
  274.7 6.4 %copy-start.4 = (s32[1,4,256]{2,1,0:T(4,128)S(1)}, s32[1,4,256]{2,1,0:T(4,128)}, u32[]{:S(2)}) copy-start(s32[1,4,256]{2,1,0:T(4,128)} %param.16) | copy-start | bytes 12292
  276.1 36.2 %all-to-all-start = ((bf16[1,1,256,3,384]{4,3,1,0,2:T(4,128)(2,1)}), bf16[1,1,256,3,384]{4,3,1,0,2:T(4,128)(2,1)}, u32[]{:S(2)}, u32[]{:S(2)}) async-start(bf16[1,1,256,3,384]{4,3,1,0,2:T(4,128)(2,1)} %copy.52), calls=%async_computation | async-start | bytes 1572864 | tf_op jit(solution)/shard_map/all_to_all | solution.py:109
  280.3 42.3 %all-gather.14.cloned.1.call-start = ((), (), s32[]{:S(2)}) async-start(), calls=%async_computation.8 | async-start | bytes 1474560 | tf_op jit(solution)/shard_map/all_gather | solution.py:60
  316.0 1.4 copy-start.3
  319.1 9.6 %all-to-all-start.1 = ((bf16[1,4,64,384]{3,2,0,1:T(8,128)(2,1)}), bf16[1,4,64,384]{3,2,0,1:T(8,128)(2,1)S(1)}, u32[]{:S(2)}, u32[]{:S(2)}) async-start(bf16[1,4,64,384]{3,2,0,1:T(8,128)(2,1)} %bitcast.30), calls=%async_computation.1 | async-start | bytes 393216 | tf_op jit(solution)/shard_map/all_to_all | solution.py:133
  322.5 43.3 %all-reduce.8.cloned.1.call-start = ((), (), s32[]{:S(2)}) async-start(), calls=%async_computation.9 | async-start | bytes 1572864 | tf_op jit(solution)/shard_map/psum | solution.py:139
Sparse Core Ops, SparseCore 0:
  8.9 53.2 all-gather.5
  63.7 29.2 all-gather.7
  95.4 36.1 all-reduce.3
  133.1 29.7 all-gather.9
  165.8 34.0 all-reduce.5
  201.4 69.9 all-gather.11
  282.8 37.2 all-gather.13
  331.6 34.1 all-reduce.7
where the time goes:
time: 376 us; the launch traced here: 375 us
  waiting for transfers between devices  322 us (86%)
  between operations  15 us (4%)
  matrix products  12.9 us (3%)
  local copies, waits for them, and re-layouts  10.5 us (3%)
  starting transfers between devices  7.84 us (2%)
  other arithmetic  6.42 us (2%)
    all_gather x1, waiting for transfers between devices, shards(): lax.all_gather(time_triple, 'tm', axis=0, tiled=True)  69.5 us
    all_gather x1, waiting for transfers between devices, shards(): lax.all_gather(cross_pairs, 'tm', axis=0, tiled=True)  50.1 us
    psum x1, waiting for transfers between devices, broadcast(): return lax.psum(block, axis)  36.6 us
    psum x1, waiting for transfers between devices, shards(): lax.psum(time_terms.astype(jnp.bfloat16), 'mp').astype(jnp.float32)  34.3 us
    psum x1, waiting for transfers between devices, shards(): lax.psum(cross_terms.astype(jnp.bfloat16), 'mp').astype(jnp.float32)  33.6 us
    all_to_all x1, waiting for transfers between devices, shards(): lax.all_to_all(triple, 'tm', split_axis=2, concat_axis=1, tiled=True)  31.1 us
    all_gather x1, waiting for transfers between devices, shards(): lax.all_gather(cross_query, 'tm', axis=0, tiled=True)  29.4 us
    all_gather x1, waiting for transfers between devices, shards(): lax.all_gather(cross_merge, 'tm', axis=1, tiled=True)  29 us
  transfers between devices with their start and end apart: 10, of which 9 were waited for; matrix products, arithmetic and copies ran while one was open for 4% of the time, Pallas kernels for 0%

commit v1 on v0

--- a/solution.py
+++ b/solution.py
@@ -4,6 +4,28 @@
 from jax.sharding import PartitionSpec as P
 
 HEAD_DIM = 64
+
+
+def joined_along(pieces, dim):
+    shape = list(pieces.shape[1:])
+    shape[dim] *= pieces.shape[0]
+    return jnp.moveaxis(pieces, 0, dim).reshape(shape)
+
+
+def grow_blocks(x, axis):
+    size = lax.axis_size(axis)
+    blocks = x[None]
+    for level in range(size.bit_length() - 1):
+        bit = 1 << level
+        other = lax.ppermute(blocks, axis, [(i, i ^ bit) for i in range(size)])
+        both = jnp.stack([blocks, other])
+        upper = lax.axis_index(axis) >> level & 1
+        blocks = jnp.where(upper == 0, both, both[::-1]).reshape(-1, *x.shape)
+    return blocks
+
+
+def doubled_up(shard, axis, dim):
+    return joined_along(grow_blocks(shard, axis), dim)
 
 
 def broadcast(block, axis, holder):
@@ -56,7 +78,7 @@
         lax.all_gather(cross_query, "tm", axis=0, tiled=True),
         lax.all_gather(cross_pairs, "tm", axis=0, tiled=True),
         lax.all_gather(cross_merge, "tm", axis=1, tiled=True),
-        lax.all_gather(time_triple, "tm", axis=0, tiled=True),
+        doubled_up(time_triple, "tm", 0),
         lax.all_gather(time_merge, "tm", axis=1, tiled=True),
     )
     flat_rows = normed.reshape(stacks * seq_tokens, model_width)

time: 376 us -> 361 us (0.960)
  waiting for transfers between devices: 322 us -> 282 us
  other arithmetic: 6.42 us -> 18.7 us
  starting transfers between devices: 7.84 us -> 18.1 us
    ppermute x0 -> x2, waiting for transfers between devices: none -> 70.6 us  [grow_blocks(): other = lax.ppermute(blocks, axis, [(i, i ^ bit) for i in range(size)])]
    all_gather x1 -> x0, waiting for transfers between devices: 69.5 us -> none  [shards(): lax.all_gather(time_triple, 'tm', axis=0, tiled=True)]
    all_gather x1, waiting for transfers between devices: 50.1 us -> 8.96 us  [shards(): lax.all_gather(cross_pairs, 'tm', axis=0, tiled=True)]
    all_gather x1, waiting for transfers between devices: 29.4 us -> 61.3 us  [shards(): lax.all_gather(cross_query, 'tm', axis=0, tiled=True)]
    psum x1, waiting for transfers between devices: 36.6 us -> 14.1 us  [broadcast(): return lax.psum(block, axis)]
    ppermute x0 -> x2, starting transfers between devices: none -> 9.79 us  [grow_blocks(): other = lax.ppermute(blocks, axis, [(i, i ^ bit) for i in range(size)])]
    select_n x0 -> x1, other arithmetic: none -> 5.85 us  [grow_blocks(): blocks = jnp.where(upper == 0, both, both[::-1]).reshape(-1, *x.shape)]
    another operation x0 -> x3, other arithmetic: none -> 5.59 us  [grow_blocks(): both = jnp.stack([blocks, other])]
  transfers between devices with their start and end apart: 10 -> 11, of which waited for: 9 -> 10; matrix products, arithmetic and copies ran while one was open for 4% -> 8% of each run, Pallas kernels for 0% -> 0%
where the time goes in v1:
time: 361 us
  waiting for transfers between devices  282 us (78%)
  other arithmetic  18.7 us (5%)
  starting transfers between devices  18.1 us (5%)
  matrix products  15.7 us (4%)
  between operations  15 us (4%)
  local copies, waits for them, and re-layouts  10.5 us (3%)
    ppermute x2, waiting for transfers between devices, grow_blocks(): other = lax.ppermute(blocks, axis, [(i, i ^ bit) for i in range(size)])  70.6 us
    all_gather x1, waiting for transfers between devices, shards(): lax.all_gather(cross_query, 'tm', axis=0, tiled=True)  61.3 us
    psum x1, waiting for transfers between devices, shards(): lax.psum(time_terms.astype(jnp.bfloat16), 'mp').astype(jnp.float32)  34.9 us
    all_to_all x1, waiting for transfers between devices, shards(): lax.all_to_all(triple, 'tm', split_axis=2, concat_axis=1, tiled=True)  30.4 us
    psum x1, waiting for transfers between devices, shards(): lax.psum(cross_terms.astype(jnp.bfloat16), 'mp').astype(jnp.float32)  28.4 us
    all_gather x1, waiting for transfers between devices, shards(): lax.all_gather(cross_merge, 'tm', axis=1, tiled=True)  26.4 us
    psum x1, waiting for transfers between devices, broadcast(): return lax.psum(block, axis)  14.1 us
    ppermute x2, starting transfers between devices, grow_blocks(): other = lax.ppermute(blocks, axis, [(i, i ^ bit) for i in range(size)])  9.79 us
  transfers between devices with their start and end apart: 11, of which 10 were waited for; matrix products, arithmetic and copies ran while one was open for 8% of the time, Pallas kernels for 0%

profile of v1, /device:TPU:0, one launch (start us, length us, event | category | flops | bytes accessed | tf_op | source)
XLA Modules:
  0.0 360.5 jit_solution(888479125646541912)
XLA Ops:
  6.5 2.1 copy.49
  8.7 3.1 collective-permute-start
  12.5 0.3 fusion.28
  12.8 0.2 convert_reduce_fusion
  13.8 0.4 fusion.6
  14.1 42.9 %collective-permute-done = bf16[1,384,3,384]{3,1,2,0:T(8,128)(2,1)S(1)} collective-permute-done((bf16[1,384,3,384]{3,1,2,0:T(8,128)(2,1)S(1)}, bf16[1,384,3,384]{3,1,2,0:T(8,128)(2,1)S(1)}, u32[]{:S(2)}, u32[]{:S(2)}) %collective-permute-start) | collective-permute-done | bytes 884768 | tf_op jit(solution)/shard_map/ppermute | solution.py:20
  57.0 0.2 pad_maximum_fusion.1
  57.2 1.7 fusion.13
  59.0 6.7 %collective-permute-start.1 = (bf16[2,384,3,384]{3,1,0,2:T(8,128)(2,1)}, bf16[2,384,3,384]{3,1,0,2:T(8,128)(2,1)}, u32[]{:S(2)}, u32[]{:S(2)}) collective-permute-start(bf16[2,384,3,384]{3,1,0,2:T(8,128)(2,1)} %get-tuple-element.21), channel_id=1, source_target_pairs={{0,8},{4,12},{8,0},{12,4},{1,9},{5,13},{9,1},{13,5},{2,10},{6,14},... | collective-permute-start | bytes 5308424 | tf_op jit(solution)/shard_map/ppermute | solution.py:20
  65.7 1.2 fusion.21
  66.9 9.0 %all-gather.5.cloned.1.call-done = bf16[1536,2,384]{2,0,1:T(8,128)(2,1)} async-done(((bf16[384,2,384]{2,0,1:T(8,128)(2,1)}), bf16[1536,2,384]{2,0,1:T(8,128)(2,1)}) %all-gather.5.cloned.1.call-update) | async-done | bytes 2359312 | tf_op jit(solution)/shard_map/all_gather | solution.py:79
  75.9 0.8 select_bitcast_fusion
  76.8 0.5 all-gather.9.cloned.1.call-update
  77.4 61.3 %all-gather.7.cloned.1.call-done = bf16[1536,384]{1,0:T(8,128)(2,1)} async-done(((bf16[384,384]{1,0:T(8,128)(2,1)}), bf16[1536,384]{1,0:T(8,128)(2,1)}) %all-gather.7.cloned.1.call-update) | async-done | bytes 1179664 | tf_op jit(solution)/shard_map/all_gather | solution.py:78
  138.6 2.1 convolution_convert_fusion.5
  140.7 0.1 copy.51
  140.9 27.7 %collective-permute-done.1 = bf16[2,384,3,384]{3,1,0,2:T(8,128)(2,1)} collective-permute-done((bf16[2,384,3,384]{3,1,0,2:T(8,128)(2,1)}, bf16[2,384,3,384]{3,1,0,2:T(8,128)(2,1)}, u32[]{:S(2)}, u32[]{:S(2)}) %collective-permute-start.1) | collective-permute-done | bytes 1769504 | tf_op jit(solution)/shard_map/ppermute | solution.py:20
  168.6 3.7 %pad_maximum_fusion = bf16[2,2,384,3,384]{4,2,1,0,3:T(8,128)(2,1)} fusion(bf16[1,2,384,3,384]{4,2,1,0,3:T(8,128)(2,1)} %bitcast.28, bf16[1,2,384,3,384]{4,2,1,0,3:T(8,128)(2,1)S(1)} %get-tuple-element.20), kind=kLoop, calls=%fused_computation.5 | loop fusion | flops 1769472 | bytes 7077888 | tf_op jit(solution)/shard_map/stack | solution.py:21
  172.2 14.1 %all-reduce.4.cloned.1.call-done = bf16[1,256,2,384]{3,1,2,0:T(8,128)(2,1)} async-done(((bf16[1,256,2,384]{3,1,2,0:T(8,128)(2,1)}), bf16[1,256,2,384]{3,1,2,0:T(8,128)(2,1)}) %all-reduce.4.cloned.1.call-update) | async-done | bytes 393232 | tf_op jit(solution)/shard_map/psum | solution.py:33
  186.3 1.1 fusion.46
  187.4 0.1 copy.50
  187.6 0.1 copy.52
  187.7 1.8 fusion.47
  189.5 1.7 convolution_convert_fusion.6
  191.2 26.4 %all-gather.9.cloned.1.call-done = bf16[384,1536]{1,0:T(8,128)(2,1)} async-done(((bf16[384,384]{1,0:T(8,128)(2,1)}), bf16[384,1536]{1,0:T(8,128)(2,1)}) %all-gather.9.cloned.1.call-update) | async-done | bytes 1179664 | tf_op jit(solution)/shard_map/all_gather | solution.py:80
  217.6 2.7 convolution_convert_fusion.2
  220.4 5.8 %reverse_select_fusion = bf16[2,2,384,3,384]{4,2,1,0,3:T(8,128)(2,1)} fusion(bf16[2,2,384,3,384]{4,2,1,0,3:T(8,128)(2,1)} %pad_maximum_fusion, pred[]{:T(512)S(6)} %eq.49), kind=kLoop, calls=%fused_computation.4 | loop fusion | flops 1769472 | bytes 7077889 | tf_op jit(solution)/shard_map/jit(_where)/select_n | solution.py:23
  226.3 28.4 %all-reduce.6.cloned.1.call-done = bf16[256,1536]{1,0:T(8,128)(2,1)} async-done(((bf16[256,1536]{1,0:T(8,128)(2,1)}), bf16[256,1536]{1,0:T(8,128)(2,1)}) %all-reduce.6.cloned.1.call-update) | async-done | bytes 786448 | tf_op jit(solution)/shard_map/psum | solution.py:119
  254.6 1.5 fusion.18
  256.2 0.4 multiply_reduce_fusion
  256.7 3.3 fusion.14
  259.9 1.4 copy.55
  261.3 4.6 %all-to-all-start = ((bf16[1,1,256,3,384]{4,3,1,0,2:T(4,128)(2,1)}), bf16[1,1,256,3,384]{4,3,1,0,2:T(4,128)(2,1)}, u32[]{:S(2)}, u32[]{:S(2)}) async-start(bf16[1,1,256,3,384]{4,3,1,0,2:T(4,128)(2,1)} %copy.55), calls=%async_computation | async-start | bytes 1572864 | tf_op jit(solution)/shard_map/all_to_all | solution.py:131
  265.9 0.6 all-gather.11.cloned.1.call-update
  266.6 30.4 %all-to-all-done = bf16[1,1,256,3,384]{4,3,1,0,2:T(4,128)(2,1)} async-done(((bf16[1,1,256,3,384]{4,3,1,0,2:T(4,128)(2,1)}), bf16[1,1,256,3,384]{4,3,1,0,2:T(4,128)(2,1)}, u32[]{:S(2)}, u32[]{:S(2)}) %all-to-all-start) | async-done | bytes 589856 | tf_op jit(solution)/shard_map/all_to_all | solution.py:131
  296.9 2.7 reshape.231
  299.7 1.1 fusion.45
  300.7 0.6 fusion.27
  301.3 0.3 copy.60
  301.8 0.3 copy.61
  302.1 0.6 fusion.15
  302.7 0.1 copy.62
  302.8 1.0 reshape.225
  303.8 3.6 all-to-all-start.1
  307.4 6.2 %all-to-all-done.1 = bf16[1,4,64,384]{3,2,0,1:T(8,128)(2,1)S(1)} async-done(((bf16[1,4,64,384]{3,2,0,1:T(8,128)(2,1)}), bf16[1,4,64,384]{3,2,0,1:T(8,128)(2,1)S(1)}, u32[]{:S(2)}, u32[]{:S(2)}) %all-to-all-start.1) | async-done | bytes 196640 | tf_op jit(solution)/shard_map/all_to_all | solution.py:155
  313.6 2.7 convolution_convert_fusion.1
  316.4 34.9 %all-reduce.8.cloned.1.call-done = bf16[256,1536]{1,0:T(8,128)(2,1)} async-done(((bf16[256,1536]{1,0:T(8,128)(2,1)}), bf16[256,1536]{1,0:T(8,128)(2,1)}) %all-reduce.8.cloned.1.call-update) | async-done | bytes 786448 | tf_op jit(solution)/shard_map/psum | solution.py:161
  351.3 2.4 fusion.10
  (36 shorter events, 0.7 us)
Async XLA Ops:
  6.5 6.0 %copy-start = (f32[8,6,1536]{2,0,1:T(8,128)S(1)}, f32[8,6,1536]{2,0,1:T(8,128)}, u32[]{:S(2)}) copy-start(f32[8,6,1536]{2,0,1:T(8,128)} %param.13) | copy-start | bytes 884740
  6.5 2.2 copy-start.3
  6.5 6.3 %copy-start.1 = (bf16[1,1,256,1536]{3,2,1,0:T(8,128)(2,1)S(1)}, bf16[1,1,256,1536]{3,2,1,0:T(8,128)(2,1)}, u32[]{:S(2)}) copy-start(bf16[1,1,256,1536]{3,2,1,0:T(8,128)(2,1)} %param.12) | copy-start | bytes 2359300
  6.5 69.3 %all-gather.5.cloned.1.call-start = ((), (), s32[]{:S(2)}) async-start(), calls=%async_computation.2 | async-start | bytes 2949120 | tf_op jit(solution)/shard_map/all_gather | solution.py:79
  8.7 130.0 %all-gather.7.cloned.1.call-start = ((), (), s32[]{:S(2)}) async-start(), calls=%async_computation.4 | async-start | bytes 1474560 | tf_op jit(solution)/shard_map/all_gather | solution.py:78
  8.7 48.3 %collective-permute-start = (bf16[1,384,3,384]{3,1,2,0:T(8,128)(2,1)S(1)}, bf16[1,384,3,384]{3,1,2,0:T(8,128)(2,1)S(1)}, u32[]{:S(2)}, u32[]{:S(2)}) collective-permute-start(bf16[1,384,3,384]{3,1,2,0:T(8,128)(2,1)S(1)} %bitcast.105), channel_id=1, source_target_pairs={{0,4},{4,0},{8,12},{12,8},{1,5},{5,1},{9,13},{13,9},{2,6},{6,2},{1... | collective-permute-start | bytes 2654216 | tf_op jit(solution)/shard_map/ppermute | solution.py:20
  11.8 174.5 %all-reduce.4.cloned.1.call-start = ((), (), s32[]{:S(2)}) async-start(), calls=%async_computation.3 | async-start | bytes 786432 | tf_op jit(solution)/shard_map/psum | solution.py:33
  59.0 109.6 %collective-permute-start.1 = (bf16[2,384,3,384]{3,1,0,2:T(8,128)(2,1)}, bf16[2,384,3,384]{3,1,0,2:T(8,128)(2,1)}, u32[]{:S(2)}, u32[]{:S(2)}) collective-permute-start(bf16[2,384,3,384]{3,1,0,2:T(8,128)(2,1)} %get-tuple-element.21), channel_id=1, source_target_pairs={{0,8},{4,12},{8,0},{12,4},{1,9},{5,13},{9,1},{13,5},{2,10},{6,14},... | collective-permute-start | bytes 5308424 | tf_op jit(solution)/shard_map/ppermute | solution.py:20
  76.7 140.9 %all-gather.9.cloned.1.call-start = ((), (), s32[]{:S(2)}) async-start(), calls=%async_computation.5 | async-start | bytes 1474560 | tf_op jit(solution)/shard_map/all_gather | solution.py:80
  77.3 177.3 %all-reduce.6.cloned.1.call-start = ((), (), s32[]{:S(2)}) async-start(), calls=%async_computation.6 | async-start | bytes 1572864 | tf_op jit(solution)/shard_map/psum | solution.py:119
  254.6 1.6 copy-start.2
  259.9 6.6 %copy-start.5 = (s32[1,4,256]{2,1,0:T(4,128)S(1)}, s32[1,4,256]{2,1,0:T(4,128)}, u32[]{:S(2)}) copy-start(s32[1,4,256]{2,1,0:T(4,128)} %param.16) | copy-start | bytes 12292
  261.3 35.6 %all-to-all-start = ((bf16[1,1,256,3,384]{4,3,1,0,2:T(4,128)(2,1)}), bf16[1,1,256,3,384]{4,3,1,0,2:T(4,128)(2,1)}, u32[]{:S(2)}, u32[]{:S(2)}) async-start(bf16[1,1,256,3,384]{4,3,1,0,2:T(4,128)(2,1)} %copy.55), calls=%async_computation | async-start | bytes 1572864 | tf_op jit(solution)/shard_map/all_to_all | solution.py:131
  265.9 41.5 %all-gather.11.cloned.1.call-start = ((), (), s32[]{:S(2)}) async-start(), calls=%async_computation.7 | async-start | bytes 1474560 | tf_op jit(solution)/shard_map/all_gather | solution.py:82
  300.7 1.4 copy-start.4
  303.8 9.8 %all-to-all-start.1 = ((bf16[1,4,64,384]{3,2,0,1:T(8,128)(2,1)}), bf16[1,4,64,384]{3,2,0,1:T(8,128)(2,1)S(1)}, u32[]{:S(2)}, u32[]{:S(2)}) async-start(bf16[1,4,64,384]{3,2,0,1:T(8,128)(2,1)} %bitcast.38), calls=%async_computation.1 | async-start | bytes 393216 | tf_op jit(solution)/shard_map/all_to_all | solution.py:155
  307.4 43.9 %all-reduce.8.cloned.1.call-start = ((), (), s32[]{:S(2)}) async-start(), calls=%async_computation.8 | async-start | bytes 1572864 | tf_op jit(solution)/shard_map/psum | solution.py:161
Sparse Core Ops, SparseCore 0:
  8.9 66.8 all-gather.4
  77.4 61.1 all-gather.6
  141.0 45.2 all-reduce.3
  187.9 29.7 all-gather.8
  220.5 34.0 all-reduce.5
  268.1 36.4 all-gather.10
  316.5 34.7 all-reduce.7
